TPU v7x, 32 devices: a whole 2x2x4 slice. The times are simulated.
32 devices in a mesh: dp: 4 (over y, x), space: 8 (over z, core).
Axes of the slice: x: 2, y: 2, z: 4, core: 2. Of those that a mesh axis runs over, the one named last changes fastest.
Arguments:
- volume: bfloat16 [4, 64, 32, 2048], P('dp', None, 'space'), may hold values from -6 to 6
- conv_weight: bfloat16 [27, 64, 128], replicated, may hold values from -0.15625 to 0.15625
- mix_weight: bfloat16 [27, 128, 256], replicated, may hold values from -0.109375 to 0.109375
- cotangent: bfloat16 [4, 8, 256, 128], P('dp', 'space'), may hold values from -6 to 6
Outputs:
- mixed_out: bfloat16 [4, 8, 256, 128], P('dp', 'space')
- mix_grad: float32 [27, 128, 256], P(None, 'space')
All inputs are finite; a program needn't handle non-finite values.
Results may differ from a plain program's by a relative error of at most 0.0049.
Values may be sent and summed in bfloat16 or wider, within the bound.
A program may use at most 64 MiB of HBM per device.

v0:
```python
import functools
import math

import jax
import jax.numpy as jnp
import numpy as np
from jax import lax
from jax.experimental import pallas as pl
from jax.experimental.pallas import tpu as pltpu
from jax.sharding import PartitionSpec as P

SY = 16
SZ = 128
JN = SY // 4
MN = SZ // 4
CELLS = JN * MN
ROWS = 16
MESH = pl.DeviceIdType.MESH


def up(value, step):
    return -(-value // step) * step


def selection():
    table = np.zeros((JN * SZ, 2, 5, JN, MN), np.float32)
    for shift in range(2):
        for v in range(5):
            for j in range(shift, JN):
                for m in range(MN):
                    z = 4 * m + v - 1
                    if z >= 0:
                        table[(j - shift) * SZ + z, shift, v, j, m] = 1.0
    return table.reshape(JN * SZ, 10 * CELLS)


def dot(a, b, dims):
    return lax.dot_general(a, b, (dims, ((), ())), preferred_element_type=jnp.float32)


def shift_m(value):
    lane = lax.broadcasted_iota(jnp.int32, value.shape, value.ndim - 1)
    return jnp.where(lane % MN == 0, 0.0, pltpu.roll(value, 1, value.ndim - 1))


def shift_j(value):
    lane = lax.broadcasted_iota(jnp.int32, value.shape, value.ndim - 1)
    return jnp.where(lane < MN, 0.0, pltpu.roll(value, MN, value.ndim - 1))


def windows(plane):
    parts = {}
    for r in range(2):
        even, odd = plane[2 * r], plane[2 * r + 1]
        odd_f = odd.astype(jnp.float32)
        before = shift_m(odd_f)
        parts[r + 1] = [before.astype(jnp.bfloat16), even, odd]
        if r == 1:
            parts[0] = [
                shift_j(before).astype(jnp.bfloat16),
                shift_j(even.astype(jnp.float32)).astype(jnp.bfloat16),
                shift_j(odd_f).astype(jnp.bfloat16),
            ]
    return parts[0] + parts[1] + parts[2]


def kernel(n, nd, scaling, vol, w1, w2, cot, sel, mixed, grad, halo, dmat, hid, rim, grp, cots, win, gsum, part, got,
           result, s_hv, s_hh, s_cot, r_cot, s_hid, r_hid, s_rs, r_rs, s_ag, r_ag):
    me = lax.axis_index("space")
    mine = lax.axis_index("dp")
    c1 = hid.shape[2]
    group = c1 // n
    span = max(group, ROWS)
    chunk = part.shape[0] // nd

    barrier = pltpu.get_barrier_semaphore()
    for d in range(1, n):
        pl.semaphore_signal(barrier, inc=1, device_id={"space": lax.rem(me + d, n)}, device_id_type=MESH)
    for d in range(1, nd):
        pl.semaphore_signal(barrier, inc=1, device_id={"dp": lax.rem(mine + d, nd)}, device_id_type=MESH)
    pl.semaphore_wait(barrier, n - 1 + nd - 1)

    above = lax.rem(me + 1, n)
    vol_copy = pltpu.make_async_remote_copy(
        vol.at[3], halo, s_hv.at[0], s_hv.at[1], device_id={"space": above}, device_id_type=MESH)
    rim_copy = pltpu.make_async_remote_copy(
        hid.at[1], rim, s_hh.at[0], s_hh.at[1], device_id={"space": above}, device_id_type=MESH)

    @pl.when(me < n - 1)
    def _():
        vol_copy.start()

    pending = []
    for d in range(1, n):
        copy = pltpu.make_async_remote_copy(
            cot, cots.at[d], s_cot.at[d], r_cot.at[d],
            device_id={"space": lax.rem(me + d, n)}, device_id_type=MESH)
        copy.start()
        pending.append(copy)

    def split(x, plane):
        rows = [
            jnp.concatenate([plane[:, (4 * j + s) * SZ : (4 * j + s + 1) * SZ] for j in range(JN)], axis=1)
            for s in range(4)
        ]
        c0 = plane.shape[0]
        flat = dot(jnp.concatenate(rows, axis=0), sel[:, : 5 * CELLS], ((1,), (0,))).astype(jnp.bfloat16)
        for s in range(4):
            dmat[x, s + 1] = flat[s * c0 : (s + 1) * c0]
        dmat[x, 0] = dot(rows[3], sel[:, 5 * CELLS :], ((1,), (0,))).astype(jnp.bfloat16)

    def first_layer(i):
        for r in range(2):
            stack = []
            for a in range(3):
                for b in range(3):
                    for c in range(3):
                        stack.append(jnp.concatenate(
                            [dmat[2 * i + a, 2 * r + b, :, v * CELLS : (v + 1) * CELLS] for v in (c, 2 + c)], axis=1))
            pre = dot(w1[...], jnp.concatenate(stack, axis=0), ((0,), (0,)))
            value = jnp.where(pre > 0, pre, 0.3 * pre).astype(jnp.bfloat16)
            for p in range(2):
                hid[i, 2 * r + p] = value[:, p * CELLS : (p + 1) * CELLS]

    def spread(i):
        for d in range(1, n):
            peer = lax.rem(me + d, n)
            start = pl.multiple_of((peer * group) // span * span, span)
            copy = pltpu.make_async_remote_copy(
                hid.at[i, :, pl.ds(start, span), :], grp.at[d, i], s_hid.at[i, d], r_hid.at[i, d],
                device_id={"space": peer}, device_id_type=MESH)
            copy.start()
            pending.append(copy)

    for x in (1, 2, 3):
        split(x + 1, vol[x])
    first_layer(1)

    @pl.when(me < n - 1)
    def _():
        rim_copy.start()

    spread(1)
    split(1, vol[0])

    @pl.when(me > 0)
    def _():
        vol_copy.wait_recv()

    @pl.when(me == 0)
    def _():
        halo[...] = jnp.zeros_like(halo)

    split(0, halo[...])
    first_layer(0)
    spread(0)

    @pl.when(me > 0)
    def _():
        rim_copy.wait_recv()

    @pl.when(me == 0)
    def _():
        rim[...] = jnp.zeros_like(rim)

    stack = []
    for plane in (rim, hid.at[0], hid.at[1]):
        stack += windows([plane[k] for k in range(4)])
    mixed[...] = dot(w2[...], jnp.concatenate(stack, axis=0), ((0,), (0,))).astype(jnp.bfloat16)

    for copy in pending:
        copy.wait_recv()
    own = pl.multiple_of((me * group) // span * span, span)
    grp[0] = hid[:, :, pl.ds(own, span), :]
    cots[0] = cot[...]
    for d in range(n):
        slab = lax.rem(me + n - d, n)
        last = windows([grp[d, 1, k] for k in range(4)])
        for k, value in enumerate(windows([grp[d, 0, k] for k in range(4)])):
            win[(9 + k) * span : (10 + k) * span, d * CELLS : (d + 1) * CELLS] = value
        for k, value in enumerate(last):
            win[(18 + k) * span : (19 + k) * span, d * CELLS : (d + 1) * CELLS] = value
        e = (d + n - 1) % n
        after = lax.rem(slab + 1, n)
        keep = jnp.where(after == 0, 0.0, 1.0)
        for k, value in enumerate(last):
            win[k * span : (k + 1) * span, e * CELLS : (e + 1) * CELLS] = (
                value.astype(jnp.float32) * keep).astype(jnp.bfloat16)
    cot_all = jnp.concatenate([cots[d] for d in range(n)], axis=1)
    total = dot(win[...], cot_all, ((1,), (1,))) * scaling
    used = total.shape[0]
    gsum[0:used] = total
    part[0:used] = total.astype(jnp.bfloat16)
    if used < part.shape[0]:
        gsum[used:] = jnp.zeros((part.shape[0] - used, total.shape[1]), jnp.float32)
        part[used:] = jnp.zeros((part.shape[0] - used, total.shape[1]), jnp.bfloat16)

    shares = []
    for d in range(1, nd):
        peer = lax.rem(mine + d, nd)
        copy = pltpu.make_async_remote_copy(
            part.at[pl.ds(pl.multiple_of(peer * chunk, ROWS), chunk)], got.at[d], s_rs.at[d], r_rs.at[d],
            device_id={"dp": peer}, device_id_type=MESH)
        copy.start()
        shares.append(copy)
    at = pl.multiple_of(mine * chunk, ROWS)
    value = gsum[pl.ds(at, chunk)]
    for d in range(1, nd):
        shares[d - 1].wait_recv()
        value = value + got[d].astype(jnp.float32)
    result[pl.ds(at, chunk)] = value.astype(jnp.bfloat16)
    gathers = []
    for d in range(1, nd):
        peer = lax.rem(mine + d, nd)
        copy = pltpu.make_async_remote_copy(
            result.at[pl.ds(at, chunk)], result.at[pl.ds(at, chunk)], s_ag.at[d], r_ag.at[d],
            device_id={"dp": peer}, device_id_type=MESH)
        copy.start()
        gathers.append(copy)
    for copy in gathers:
        copy.wait_recv()
    for k in range(27):
        grad[k] = result[k * span : (k + 1) * span].astype(jnp.float32)

    for copy in pending + shares + gathers:
        copy.wait_send()

    @pl.when(me < n - 1)
    def _():
        vol_copy.wait_send()
        rim_copy.wait_send()


def on_device(n, nd, volume, conv_weight, mix_weight, cotangent):
    c0, c1, c2 = volume.shape[1], conv_weight.shape[2], mix_weight.shape[2]
    group = c1 // n
    span = max(group, ROWS)
    scaling = 1.0 / math.sqrt(nd * n * cotangent.shape[1] * CELLS)
    used = 27 * span
    chunk = up(-(-used // nd), ROWS)
    vol = volume[0].transpose(1, 0, 2)
    sel = jnp.asarray(selection(), jnp.bfloat16)
    bf16, f32 = jnp.bfloat16, jnp.float32
    dma = pltpu.SemaphoreType.DMA
    mixed, grad = pl.pallas_call(
        functools.partial(kernel, n, nd, scaling),
        name="conv_pair",
        out_shape=(jax.ShapeDtypeStruct((c2, CELLS), bf16), jax.ShapeDtypeStruct((27, span, c2), f32)),
        in_specs=[pl.BlockSpec(memory_space=pltpu.VMEM)] * 5,
        out_specs=(pl.BlockSpec(memory_space=pltpu.VMEM),) * 2,
        scratch_shapes=[
            pltpu.VMEM((c0, SY * SZ), bf16),
            pltpu.VMEM((5, 5, c0, 5 * CELLS), bf16),
            pltpu.VMEM((2, 4, c1, CELLS), bf16),
            pltpu.VMEM((4, c1, CELLS), bf16),
            pltpu.VMEM((n, 2, 4, span, CELLS), bf16),
            pltpu.VMEM((n, c2, CELLS), bf16),
            pltpu.VMEM((used, n * CELLS), bf16),
            pltpu.VMEM((nd * chunk, c2), f32),
            pltpu.VMEM((nd * chunk, c2), bf16),
            pltpu.VMEM((nd, chunk, c2), bf16),
            pltpu.VMEM((nd * chunk, c2), bf16),
            dma((2,)), dma((2,)), dma((n,)), dma((n,)), dma((2, n)), dma((2, n)),
            dma((nd,)), dma((nd,)), dma((nd,)), dma((nd,)),
        ],
        compiler_params=pltpu.CompilerParams(collective_id=0, has_side_effects=True, vmem_limit_bytes=56 * 2**20),
    )(vol, conv_weight.reshape(27 * c0, c1), mix_weight.reshape(27 * c1, c2), cotangent[0, 0], sel)
    if span > group:
        grad = lax.dynamic_slice_in_dim(grad, lax.axis_index("space") * group % span, group, axis=1)
    return mixed[None, None], grad


def solution(mesh):
    return jax.shard_map(
        functools.partial(on_device, mesh.shape["space"], mesh.shape["dp"]),
        mesh=mesh,
        in_specs=(P("dp", None, "space", None), P(), P(), P("dp", "space", None, None)),
        out_specs=(P("dp", "space", None, None), P(None, "space", None)),
        check_vma=False,
    )
```

profile of v0, /device:TPU:24, one launch (start us, length us, event | category | flops | bytes accessed | tf_op | source)
XLA Modules:
  0.0 45.3 jit_solution(18372347049149360790)
XLA Ops:
  0.6 2.8 %copy.9 = bf16[1,64,4,2048]{3,1,2,0:T(8,128)(2,1)} copy(bf16[1,64,4,2048]{3,2,1,0:T(4,128)(2,1)} %param.5) | data formatting | bytes 2097152 | tf_op args[0]
  3.4 38.6 %conv_pair.1 = (bf16[256,128]{1,0:T(8,128)(2,1)}, f32[27,16,256]{2,1,0:T(8,128)}) custom-call(bf16[4,64,2048]{2,1,0:T(8,128)(2,1)} %bitcast.9, bf16[1728,128]{1,0:T(8,128)(2,1)} %bitcast.11, bf16[3456,256]{1,0:T(8,128)(2,1)} %bitcast.10, bf16[256,128]{1,0:T(8,128)(2,1)} %bitcast.12, bf16[512,1280]{1,0:T(8,128)(2,1)} %constant.2.clone.sel), custom_call_target="tpu_custom_call" | custom-call | tf_op jit(solution)/shard_map/conv_pair/pallas_call | solution.py:245
  42.0 1.5 %copy.12 = bf16[1,1,256,128]{3,2,1,0:T(8,128)(2,1)} copy(bf16[1,1,256,128]{3,2,1,0:T(8,128)(2,1)} %bitcast.13) | data formatting | bytes 131072
  43.5 1.8 %copy.13 = f32[27,16,256]{2,1,0:T(8,128)} copy(f32[27,16,256]{2,1,0:T(8,128)} %get-tuple-element.9) | data formatting | bytes 884736
where the time goes:
time: 45.5 us; the launch traced here: 45.3 us
  Pallas kernels  38.6 us (85%)
  local copies, waits for them, and re-layouts  6.07 us (13%)
  between operations  0.64 us (1%)
    pallas_call x1, Pallas kernels, on_device(): pl.pallas_call(functools.partial(kernel, n, nd, scaling), name='conv_pair...  38.6 us
    unnamed x3, local copies, waits for them, and re-layouts  6.07 us

commit v1 on v0

v1 whole, which is shorter than its diff:
```python
import functools
import math

import jax
import jax.numpy as jnp
import numpy as np
from jax import lax
from jax.experimental import pallas as pl
from jax.experimental.pallas import tpu as pltpu
from jax.sharding import PartitionSpec as P

SY = 16
SZ = 128
JN = SY // 4
MN = SZ // 4
CELLS = JN * MN
ROWS = 16
MESH = pl.DeviceIdType.MESH


def up(value, step):
    return -(-value // step) * step


def selection():
    table = np.zeros((JN * SZ, 2, 5, JN, MN), np.float32)
    for shift in range(2):
        for v in range(5):
            for j in range(shift, JN):
                for m in range(MN):
                    z = 4 * m + v - 1
                    if z >= 0:
                        table[(j - shift) * SZ + z, shift, v, j, m] = 1.0
    return table.reshape(JN * SZ, 10 * CELLS)


def dot(a, b, dims):
    return lax.dot_general(a, b, (dims, ((), ())), preferred_element_type=jnp.float32)


def shift_m(value):
    lane = lax.broadcasted_iota(jnp.int32, value.shape, value.ndim - 1)
    return jnp.where(lane % MN == 0, 0.0, pltpu.roll(value, 1, value.ndim - 1))


def shift_j(value):
    lane = lax.broadcasted_iota(jnp.int32, value.shape, value.ndim - 1)
    return jnp.where(lane < MN, 0.0, pltpu.roll(value, MN, value.ndim - 1))


def windows(plane):
    parts = {}
    for r in range(2):
        even, odd = plane[2 * r], plane[2 * r + 1]
        odd_f = odd.astype(jnp.float32)
        before = shift_m(odd_f)
        parts[r + 1] = [before.astype(jnp.bfloat16), even, odd]
        if r == 1:
            parts[0] = [
                shift_j(before).astype(jnp.bfloat16),
                shift_j(even.astype(jnp.float32)).astype(jnp.bfloat16),
                shift_j(odd_f).astype(jnp.bfloat16),
            ]
    return parts[0] + parts[1] + parts[2]


def kernel(n, nd, scaling, vol_in, w1_in, w2_in, cot_in, sel_in, mixed, grad, vol, w1, w2, sel, halo, dmat, hid, rim, grp,
           cots, win, gsum, part, got, result, s_in, s_hv, s_hh, r_cot, s_cot, s_hid, r_hid, s_rs, r_rs, s_ag, r_ag):
    me = lax.axis_index("space")
    mine = lax.axis_index("dp")
    z, core = me // 2, me % 2
    chips = n // 2
    sibling = 2 * z + 1 - core
    c1 = hid.shape[2]
    group = c1 // n
    span = max(group, ROWS)

    loads = [
        pltpu.make_async_copy(src, dst, s_in.at[k])
        for k, (src, dst) in enumerate(
            ((vol_in, vol), (sel_in, sel), (w1_in, w1), (w2_in, w2), (cot_in, cots.at[me])))
    ]
    for load in loads:
        load.start()

    barrier = pltpu.get_barrier_semaphore()
    for d in range(1, n):
        pl.semaphore_signal(barrier, inc=1, device_id={"space": lax.rem(me + d, n)}, device_id_type=MESH)
    for d in range(1, nd):
        pl.semaphore_signal(barrier, inc=1, device_id={"dp": lax.rem(mine + d, nd)}, device_id_type=MESH)
    pl.semaphore_wait(barrier, n - 1 + nd - 1)

    above = lax.rem(me + 1, n)
    vol_copy = pltpu.make_async_remote_copy(
        vol_in.at[3], halo, s_hv.at[0], s_hv.at[1], device_id={"space": above}, device_id_type=MESH)
    rim_copy = pltpu.make_async_remote_copy(
        hid.at[1], rim, s_hh.at[0], s_hh.at[1], device_id={"space": above}, device_id_type=MESH)

    @pl.when(me < n - 1)
    def _():
        vol_copy.start()

    def cot_hop(block, source, target, way, h):
        return pltpu.make_async_remote_copy(
            block, cots.at[source], s_cot.at[way, h], r_cot.at[source],
            device_id={"space": target}, device_id_type=MESH)

    def relay(block, h, finish):
        act = (lambda copy: copy.wait_send()) if finish else (lambda copy: copy.start())
        lower, upper = (me + n - 2 * h) % n, (me + 2 * h) % n

        @pl.when(z >= h)
        def _():
            if h > 0 and not finish:
                cot_hop(block(lower), lower, sibling, 0, h).wait_recv()
            act(cot_hop(block(lower), lower, sibling, 0, h))

            @pl.when(z + 1 < chips)
            def _():
                act(cot_hop(block(lower), lower, (me + 2) % n, 1, h))

        @pl.when(z + h < chips)
        def _():
            if h > 0:
                if not finish:
                    cot_hop(block(upper), upper, sibling, 2, h).wait_recv()
                act(cot_hop(block(upper), upper, sibling, 2, h))

            @pl.when(z >= 1)
            def _():
                act(cot_hop(block(upper), upper, (me + n - 2) % n, 3, h))

    def block_of(h):
        return (lambda source: cot_in) if h == 0 else (lambda source: cots.at[source])

    relay(block_of(0), 0, False)

    def split(x, plane):
        rows = [
            jnp.concatenate([plane[:, (4 * j + s) * SZ : (4 * j + s + 1) * SZ] for j in range(JN)], axis=1)
            for s in range(4)
        ]
        c0 = plane.shape[0]
        flat = dot(jnp.concatenate(rows, axis=0), sel[:, : 5 * CELLS], ((1,), (0,))).astype(jnp.bfloat16)
        for s in range(4):
            dmat[x, s + 1] = flat[s * c0 : (s + 1) * c0]
        dmat[x, 0] = dot(rows[3], sel[:, 5 * CELLS :], ((1,), (0,))).astype(jnp.bfloat16)

    def first_layer(i):
        for r in range(2):
            stack = []
            for a in range(3):
                for b in range(3):
                    for c in range(3):
                        stack.append(jnp.concatenate(
                            [dmat[2 * i + a, 2 * r + b, :, v * CELLS : (v + 1) * CELLS] for v in (c, 2 + c)], axis=1))
            pre = dot(w1[...], jnp.concatenate(stack, axis=0), ((0,), (0,)))
            value = jnp.where(pre > 0, pre, 0.3 * pre).astype(jnp.bfloat16)
            for p in range(2):
                hid[i, 2 * r + p] = value[:, p * CELLS : (p + 1) * CELLS]

    own = pl.multiple_of((me * group) // span * span, span)

    def piece(i, d):
        peer = (me + d) % n
        start = pl.multiple_of((peer * group) // span * span, span)
        return pltpu.make_async_remote_copy(
            hid.at[i, :, pl.ds(start, span), :], grp.at[me, i], s_hid.at[i, d], r_hid.at[i, me],
            device_id={"space": peer}, device_id_type=MESH)

    def spread(i):
        for d in range(1, n):
            piece(i, d).start()
        grp[me, i] = hid[i, :, pl.ds(own, span), :]

    def collect(i):
        for d in range(1, n):
            source = (me + d) % n
            pltpu.make_async_remote_copy(
                hid.at[i, :, pl.ds(own, span), :], grp.at[source, i], s_hid.at[i, d], r_hid.at[i, source],
                device_id={"space": source}, device_id_type=MESH).wait_recv()

    loads[0].wait()
    loads[1].wait()
    for x in (1, 2, 3):
        split(x + 1, vol[x])
    loads[2].wait()
    first_layer(1)

    @pl.when(me < n - 1)
    def _():
        rim_copy.start()

    spread(1)
    split(1, vol[0])
    hops = list(range(1, chips))
    if hops:
        relay(block_of(1), 1, False)

    @pl.when(me > 0)
    def _():
        vol_copy.wait_recv()

    @pl.when(me == 0)
    def _():
        halo[...] = jnp.zeros_like(halo)

    split(0, halo[...])
    first_layer(0)
    spread(0)
    for h in hops[1:2]:
        relay(block_of(h), h, False)

    @pl.when(me > 0)
    def _():
        rim_copy.wait_recv()

    @pl.when(me == 0)
    def _():
        rim[...] = jnp.zeros_like(rim)

    stack = []
    for plane in (rim, hid.at[0], hid.at[1]):
        stack += windows([plane[k] for k in range(4)])
    loads[3].wait()
    mixed[...] = dot(w2[...], jnp.concatenate(stack, axis=0), ((0,), (0,))).astype(jnp.bfloat16)
    for h in hops[2:]:
        relay(block_of(h), h, False)

    def columns(s):
        return slice(s * CELLS, (s + 1) * CELLS)

    nine = 9 * span
    zero = jnp.zeros((span, CELLS), jnp.bfloat16)
    collect(1)
    for s in range(n):
        for k, value in enumerate(windows([grp[s, 1, q] for q in range(4)])):
            win[nine + k * span : nine + (k + 1) * span, columns(s)] = value
            if s < n - 1:
                win[k * span : (k + 1) * span, columns(s + 1)] = value
    for k in range(9):
        win[k * span : (k + 1) * span, columns(0)] = zero
    loads[4].wait()
    for d in range(chips):
        source = 2 * ((z + d) % chips) + 1 - core
        cot_hop(cots.at[source], source, sibling, 0, 0).wait_recv()
    cot_all = jnp.concatenate([cots[s] for s in range(n)], axis=1)

    bounds = (2 * nine, nine)
    chunks = [up(-(-bound // nd), ROWS) for bound in bounds]
    base = (0, nd * chunks[0])

    def share(t, d):
        peer = (mine + d) % nd
        at = pl.multiple_of(base[t] + peer * chunks[t], ROWS)
        return pltpu.make_async_remote_copy(
            part.at[pl.ds(at, chunks[t])], got.at[t, d, pl.ds(0, chunks[t])], s_rs.at[t, d], r_rs.at[t, d],
            device_id={"dp": peer}, device_id_type=MESH)

    def publish(t, d):
        at = pl.multiple_of(base[t] + mine * chunks[t], ROWS)
        return pltpu.make_async_remote_copy(
            result.at[pl.ds(at, chunks[t])], result.at[pl.ds(at, chunks[t])], s_ag.at[t, d], r_ag.at[t, d],
            device_id={"dp": (mine + d) % nd}, device_id_type=MESH)

    def total(t):
        first, count = (0, 2 * nine) if t == 0 else (2 * nine, nine)
        value = dot(win[first : first + count], cot_all, ((1,), (1,))) * scaling
        gsum[base[t] : base[t] + count] = value
        part[base[t] : base[t] + count] = value.astype(jnp.bfloat16)
        rest = nd * chunks[t] - count
        if rest:
            gsum[base[t] + count : base[t] + count + rest] = jnp.zeros((rest, value.shape[1]), jnp.float32)
            part[base[t] + count : base[t] + count + rest] = jnp.zeros((rest, value.shape[1]), jnp.bfloat16)
        for d in range(1, nd):
            share(t, d).start()

    def reduce(t):
        at = pl.multiple_of(base[t] + mine * chunks[t], ROWS)
        value = gsum[pl.ds(at, chunks[t])]
        for d in range(1, nd):
            share(t, d).wait_recv()
            value = value + got[t, d, : chunks[t]].astype(jnp.float32)
        result[pl.ds(at, chunks[t])] = value.astype(jnp.bfloat16)
        for d in range(1, nd):
            publish(t, d).start()

    total(0)
    collect(0)
    for s in range(n):
        for k, value in enumerate(windows([grp[s, 0, q] for q in range(4)])):
            win[2 * nine + k * span : 2 * nine + (k + 1) * span, columns(s)] = value
    total(1)
    reduce(0)
    reduce(1)
    for t, taps in ((0, [*range(9), *range(18, 27)]), (1, range(9, 18))):
        for d in range(1, nd):
            at = pl.multiple_of(base[t] + ((mine + nd - d) % nd) * chunks[t], ROWS)
            pltpu.make_async_remote_copy(
                result.at[pl.ds(at, chunks[t])], result.at[pl.ds(at, chunks[t])], s_ag.at[t, d], r_ag.at[t, d],
                device_id={"dp": (mine + d) % nd}, device_id_type=MESH).wait_recv()
        for k, tap in enumerate(taps):
            grad[tap] = result[base[t] + k * span : base[t] + (k + 1) * span].astype(jnp.float32)

    for i in range(2):
        for d in range(1, n):
            piece(i, d).wait_send()
        for d in range(1, nd):
            share(i, d).wait_send()
            publish(i, d).wait_send()
    for h in range(chips):
        relay(block_of(h), h, True)

    @pl.when(me < n - 1)
    def _():
        vol_copy.wait_send()
        rim_copy.wait_send()


def on_device(n, nd, volume, conv_weight, mix_weight, cotangent):
    c0, c1, c2 = volume.shape[1], conv_weight.shape[2], mix_weight.shape[2]
    group = c1 // n
    span = max(group, ROWS)
    scaling = 1.0 / math.sqrt(nd * n * cotangent.shape[1] * CELLS)
    used = 27 * span
    chunks = [up(-(-part // nd), ROWS) for part in (18 * span, 9 * span)]
    padded = nd * sum(chunks)
    vol = volume[0].transpose(1, 0, 2)
    sel = jnp.asarray(selection(), jnp.bfloat16)
    bf16, f32 = jnp.bfloat16, jnp.float32
    dma = pltpu.SemaphoreType.DMA
    mixed, grad = pl.pallas_call(
        functools.partial(kernel, n, nd, scaling),
        name="conv_pair",
        out_shape=(jax.ShapeDtypeStruct((c2, CELLS), bf16), jax.ShapeDtypeStruct((27, span, c2), f32)),
        in_specs=[pl.BlockSpec(memory_space=pl.ANY)] * 5,
        out_specs=(pl.BlockSpec(memory_space=pltpu.VMEM),) * 2,
        scratch_shapes=[
            pltpu.VMEM(vol.shape, bf16),
            pltpu.VMEM((27 * c0, c1), bf16),
            pltpu.VMEM((27 * c1, c2), bf16),
            pltpu.VMEM(sel.shape, bf16),
            pltpu.VMEM((c0, SY * SZ), bf16),
            pltpu.VMEM((5, 5, c0, 5 * CELLS), bf16),
            pltpu.VMEM((2, 4, c1, CELLS), bf16),
            pltpu.VMEM((4, c1, CELLS), bf16),
            pltpu.VMEM((n, 2, 4, span, CELLS), bf16),
            pltpu.VMEM((n, c2, CELLS), bf16),
            pltpu.VMEM((used, n * CELLS), bf16),
            pltpu.VMEM((padded, c2), f32),
            pltpu.VMEM((padded, c2), bf16),
            pltpu.VMEM((2, nd, chunks[0], c2), bf16),
            pltpu.VMEM((padded, c2), bf16),
            dma((5,)), dma((2,)), dma((2,)), dma((n,)), dma((4, n // 2)), dma((2, n)), dma((2, n)),
            dma((2, nd)), dma((2, nd)), dma((2, nd)), dma((2, nd)),
        ],
        compiler_params=pltpu.CompilerParams(collective_id=0, has_side_effects=True, vmem_limit_bytes=56 * 2**20),
    )(vol, conv_weight.reshape(27 * c0, c1), mix_weight.reshape(27 * c1, c2), cotangent[0, 0], sel)
    if span > group:
        grad = lax.dynamic_slice_in_dim(grad, lax.axis_index("space") * group % span, group, axis=1)
    return mixed[None, None], grad


def solution(mesh):
    return jax.shard_map(
        functools.partial(on_device, mesh.shape["space"], mesh.shape["dp"]),
        mesh=mesh,
        in_specs=(P("dp", None, "space", None), P(), P(), P("dp", "space", None, None)),
        out_specs=(P("dp", "space", None, None), P(None, "space", None)),
        check_vma=False,
    )
```

time: 45.5 us -> 37.9 us (0.83)
  the two profiles are of different devices: /device:TPU:24 before, /device:TPU:0 now
where the time goes in v1:
time: 37.9 us; the launch traced here: 37.7 us
  Pallas kernels  31 us (82%)
  local copies, waits for them, and re-layouts  6.07 us (16%)
  between operations  0.64 us (2%)
    pallas_call x1, Pallas kernels, on_device(): pl.pallas_call(functools.partial(kernel, n, nd, scaling), name='conv_pair...  31 us
    unnamed x3, local copies, waits for them, and re-layouts  6.07 us

profile of v1, /device:TPU:0, one launch (start us, length us, event | category | flops | bytes accessed | tf_op | source)
XLA Modules:
  0.0 37.7 jit_solution(16708999414928155325)
XLA Ops:
  0.6 2.8 %copy.9 = bf16[1,64,4,2048]{3,1,2,0:T(8,128)(2,1)} copy(bf16[1,64,4,2048]{3,2,1,0:T(4,128)(2,1)} %param.5) | data formatting | bytes 2097152 | tf_op args[0]
  3.4 31.0 %conv_pair.1 = (bf16[256,128]{1,0:T(8,128)(2,1)}, f32[27,16,256]{2,1,0:T(8,128)}) custom-call(bf16[4,64,2048]{2,1,0:T(8,128)(2,1)} %bitcast.9, bf16[1728,128]{1,0:T(8,128)(2,1)} %bitcast.11, bf16[3456,256]{1,0:T(8,128)(2,1)} %bitcast.10, bf16[256,128]{1,0:T(8,128)(2,1)} %bitcast.12, bf16[512,1280]{1,0:T(8,128)(2,1)} %constant.2.clone.sel_in), custom_call_target="tpu_custom_call" | custom-call | tf_op jit(solution)/shard_map/conv_pair/pallas_call | solution.py:332
  34.4 1.5 %copy.12 = bf16[1,1,256,128]{3,2,1,0:T(8,128)(2,1)} copy(bf16[1,1,256,128]{3,2,1,0:T(8,128)(2,1)} %bitcast.13) | data formatting | bytes 131072
  35.9 1.8 %copy.13 = f32[27,16,256]{2,1,0:T(8,128)} copy(f32[27,16,256]{2,1,0:T(8,128)} %get-tuple-element.9) | data formatting | bytes 884736
